TPU v7x, 32 devices: a whole 2x2x4 slice. The times are simulated.
32 devices in a mesh: row: 8 (over z, x), col: 4 (over y, core).
Axes of the slice: x: 2, y: 2, z: 4, core: 2. Of those that a mesh axis runs over, the one named last changes fastest.
Arguments:
- start_block: float32 [8, 32768], P(None, ('row', 'col')), may hold values from -6 to 6
- blocks: bfloat16 [8, 4, 128, 128, 128], P('row', 'col'), as said below
- block_rows: int32 [8, 4, 128], P(None, 'col'), may hold values from 0 to 31, as said below
- block_cols: int32 [8, 4, 128], P(None, 'col'), may hold values from 0 to 63, as said below
- counts: int32 [8, 4], replicated, may hold values from 1 to 128, as said below
Outputs:
- next_block: float32 [8, 32768], P(None, ('row', 'col'))
- tridiagonal: float32 [16, 16], replicated
Inputs may be any that keep to these rules, and one draw needn't show every extreme that they name: `block_rows`: entries of each tile are local block rows below 32; within a tile the used slots name distinct blocks whose global row block is at or after the global column block; slots at or after counts are 0 and not part of H. `block_cols`: local block columns below 64, paired with block_rows; unused slots are 0. `counts`: some tile holds exactly 128 blocks in every draw. Blocks whose global row and column blocks agree are symmetric.
All inputs are finite; a program needn't handle non-finite values.
Results may differ from a plain program's by a relative error of at most 0.0048.
Values may be sent and summed in bfloat16 or wider, within the bound.
No kernel may reach another device: no remote copies, remote signals or barrier semaphores. Data moves between devices by JAX's collectives and lax.ppermute only.
A program may use at most 64 MiB of HBM per device.

v0:
```python
import math
import jax
import jax.numpy as jnp
from jax import lax
from jax.sharding import PartitionSpec as P

ITERS = 2
blocks_per_step = 16


def accumulate(
    stored,
    row_list,
    col_list,
    first_slot,
    live_count,
    tile_row,
    tile_col,
    shape_info,
    row_vector,
    col_vector,
    totals,
):
    row_blocks, col_blocks, piece_blocks, grid_cols = shape_info
    vectors = row_vector.shape[0]
    block_side = stored.shape[-1]
    slot_total = stored.shape[0]
    row_pieces = row_vector.reshape(vectors, row_blocks, block_side)
    col_pieces = col_vector.reshape(vectors, col_blocks, block_side)
    offsets = jnp.arange(blocks_per_step, dtype=jnp.int32)
    row_range = jnp.arange(row_blocks, dtype=jnp.int32)
    col_range = jnp.arange(col_blocks, dtype=jnp.int32)

    def visit(group_index, running):
        row_total, col_total = running
        local_slot = group_index * blocks_per_step + offsets
        is_valid = local_slot < live_count
        slot_ids = jnp.clip(first_slot + local_slot, 0, slot_total - 1)
        tile_data = jnp.take(stored, slot_ids, axis=0)
        row_ids = jnp.take(row_list, slot_ids)
        col_ids = jnp.take(col_list, slot_ids)
        global_row = tile_row * row_blocks + row_ids
        global_col = (
            col_ids // piece_blocks * grid_cols + tile_col
        ) * piece_blocks + col_ids % piece_blocks
        mirror = is_valid & (global_row != global_col)
        col_taken = jnp.take(col_pieces, col_ids, axis=1)
        row_taken = jnp.take(row_pieces, row_ids, axis=1)
        direct = jnp.einsum(
            "gij,kgj->kgi", tile_data, col_taken, preferred_element_type=jnp.float32
        )
        turned = jnp.einsum(
            "gji,kgj->kgi", tile_data, row_taken, preferred_element_type=jnp.float32
        )
        pick_rows = ((row_ids[:, None] == row_range[None, :]) & is_valid[:, None]).astype(
            jnp.float32
        )
        pick_cols = ((col_ids[:, None] == col_range[None, :]) & mirror[:, None]).astype(jnp.float32)
        row_total = row_total + jnp.einsum(
            "gs,kgi->ksi", pick_rows, direct, precision=lax.Precision.HIGHEST
        )
        col_total = col_total + jnp.einsum(
            "gs,kgi->ksi", pick_cols, turned, precision=lax.Precision.HIGHEST
        )
        return (row_total, col_total)

    group_count = (live_count + blocks_per_step - 1) // blocks_per_step
    return lax.fori_loop(0, group_count, visit, totals)


def per_device(start_block, blocks, block_rows, block_cols, counts):
    highest = lax.Precision.HIGHEST
    vectors, piece_len = start_block.shape
    stored = blocks[0, 0]
    block_side = stored.shape[-1]
    grid_rows = lax.axis_size("row")
    grid_cols = lax.axis_size("col")
    piece_blocks = piece_len // block_side
    row_blocks = grid_cols * piece_blocks
    col_blocks = grid_rows * piece_blocks
    shape_info = (row_blocks, col_blocks, piece_blocks, grid_cols)
    tile_row = lax.axis_index("row")
    tile_col = lax.axis_index("col")
    row_lists = block_rows[:, 0, :]
    col_lists = block_cols[:, 0, :]
    own_count = counts[tile_row, tile_col]
    own_rows = row_lists[tile_row]
    own_cols = col_lists[tile_row]
    start_sum = lax.psum(jnp.dot(start_block, start_block.T, precision=highest), ("row", "col"))
    factor = jnp.linalg.cholesky(start_sum)
    current = lax.linalg.triangular_solve(factor, start_block, left_side=True, lower=True)
    previous = current
    prev_factor = factor
    diagonals = []
    couplings = []
    for step_index in range(ITERS):
        half_block = current.astype(jnp.bfloat16)
        row_vector = lax.all_gather(half_block, "col", axis=1, tiled=True)
        col_vector = lax.all_gather(half_block, "row", axis=1, tiled=True)
        row_zero = jnp.zeros((vectors, row_blocks, block_side), jnp.float32)
        col_zero = jnp.zeros((vectors, col_blocks, block_side), jnp.float32)
        row_total, col_total = accumulate(
            stored,
            own_rows,
            own_cols,
            0,
            own_count,
            tile_row,
            tile_col,
            shape_info,
            row_vector,
            col_vector,
            (row_zero, col_zero),
        )
        row_part = lax.psum_scatter(
            row_total.reshape(vectors, row_blocks * block_side),
            "col",
            scatter_dimension=1,
            tiled=True,
        )
        col_part = lax.psum_scatter(
            col_total.reshape(vectors, col_blocks * block_side),
            "row",
            scatter_dimension=1,
            tiled=True,
        )
        image = row_part + col_part
        if step_index > 0:
            image = image - jnp.dot(prev_factor.T, previous, precision=highest)
        local_proj = jnp.dot(current, image.T, precision=highest)
        local_square = jnp.dot(image, image.T, precision=highest)
        projection, squares = lax.psum((local_proj, local_square), ("row", "col"))
        image = image - jnp.dot(projection.T, current, precision=highest)
        gram = squares - jnp.dot(projection.T, projection, precision=highest)
        factor = jnp.linalg.cholesky(gram)
        following = lax.linalg.triangular_solve(factor, image, left_side=True, lower=True)
        diagonals.append(projection)
        couplings.append(factor)
        previous, prev_factor, current = (current, factor, following)
    tri_size = ITERS * vectors
    tridiagonal = jnp.zeros((tri_size, tri_size), jnp.float32)
    for step_index in range(ITERS):
        low = step_index * vectors
        tridiagonal = tridiagonal.at[low : low + vectors, low : low + vectors].set(
            diagonals[step_index]
        )
        if step_index + 1 < ITERS:
            tridiagonal = tridiagonal.at[
                low : low + vectors, low + vectors : low + 2 * vectors
            ].set(couplings[step_index])
            tridiagonal = tridiagonal.at[
                low + vectors : low + 2 * vectors, low : low + vectors
            ].set(couplings[step_index].T)
    order_root = math.sqrt(piece_len * grid_rows * grid_cols)
    return (current * order_root, tridiagonal)


def solution(mesh):
    placed = (
        P(None, ("row", "col")),
        P("row", "col", None, None, None),
        P(None, "col", None),
        P(None, "col", None),
        P(),
    )
    return jax.shard_map(
        per_device,
        mesh=mesh,
        in_specs=placed,
        out_specs=(P(None, ("row", "col")), P()),
        check_vma=False,
    )
```

profile of v0, /device:TPU:0, one launch (start us, length us, event | category | flops | bytes accessed | tf_op | source)
XLA Modules:
  0.0 520.5 jit_solution(15743571645493684998)
XLA Ops:
  7.2 1.3 dynamic_slice.9
  9.4 41.9 %psum.35 = f32[8,8]{0,1:T(8,128)S(1)} all-reduce(f32[8,8]{0,1:T(8,128)S(1)} %fusion.100), channel_id=1, replica_groups=mesh['row'=8,'col'=4] {'row','col'}, use_global_device_ids=true, to_apply=%region_0.0 | all-reduce | flops 64 | bytes 512 | tf_op jit(solution)/shard_map/psum | solution.py:89
  51.5 0.7 cholesky.59
  54.4 5.5 %all_gather.13 = bf16[8,4096]{1,0:T(8,128)(2,1)S(1)} all-gather(bf16[8,1024]{1,0:T(8,128)(2,1)S(1)} %get-tuple-element.597), channel_id=1, replica_groups=mesh['row'=8,'col'=4] {'col'}, dimensions={1}, use_global_device_ids=true | all-gather | bytes 81920 | tf_op jit(solution)/shard_map/all_gather | solution.py:98
  59.9 30.5 %all_gather.12 = bf16[8,8192]{1,0:T(8,128)(2,1)S(1)} all-gather(bf16[8,1024]{1,0:T(8,128)(2,1)S(1)} %get-tuple-element.597), channel_id=1, replica_groups=mesh['row'=8,'col'=4] {'row'}, dimensions={1}, use_global_device_ids=true | all-gather | bytes 147456 | tf_op jit(solution)/shard_map/all_gather | solution.py:99
  90.4 0.7 dynamic-slice_bitcast_fusion
  91.1 7.7 %while.34 = (s32[]{:T(128)}, f32[8,32,128]{2,1,0:T(8,128)S(1)}, f32[8,64,128]{2,1,0:T(8,128)S(1)}, s32[]{:T(128)}, s32[128]{0:T(128)S(1)}, /*index=5*/bf16[8,64,...) while((s32[]{:T(128)}, f32[8,32,128]{2,1,0:T(8,128)S(1)}, ...), condition=%wide.region_4.11_spmd.clone, body=%wide.region_3.10_spmd.clone.sunk | while | flops 27925444 | bytes 3356565 | solution.py:68
  92.5 0.7 compare_and_fusion.14
  94.4 2.8 gather_fusion
  98.8 0.7 copy.71
  99.6 0.8 copy.69
  100.6 0.7 and_reduce_fusion
  101.9 71.0 %reduce-scatter.5.cloned.1.call-done = f32[8,1024]{1,0:T(8,128)} async-done(((f32[8,4096]{1,0:T(8,128)}), f32[8,1024]{1,0:T(8,128)}) %reduce-scatter.5.cloned.1.call-update) | async-done | bytes 32784 | tf_op jit(solution)/shard_map/reduce_scatter | solution.py:115
  172.9 65.4 %reduce-scatter.7.cloned.1.call-done = f32[8,1024]{1,0:T(8,128)} async-done(((f32[8,8192]{1,0:T(8,128)}), f32[8,1024]{1,0:T(8,128)}) %reduce-scatter.7.cloned.1.call-update) | async-done | bytes 32784 | tf_op jit(solution)/shard_map/reduce_scatter | solution.py:121
  238.3 0.8 add.228
  239.4 40.2 %all-reduce.2 = (f32[8,8]{1,0:T(8,128)S(1)}, f32[8,8]{0,1:T(8,128)S(1)}) all-reduce(f32[8,8]{1,0:T(8,128)S(1)} %fusion.102, f32[8,8]{0,1:T(8,128)S(1)} %fusion.101), channel_id=1, replica_groups=mesh['row'=8,'col'=4] {'row','col'}, use_global_device_ids=true, to_apply=%region_8.15 | all-reduce | flops 128 | bytes 1024 | tf_op jit(solution)/shard_map/psum | solution.py:132
  280.1 0.7 cholesky.70
  281.5 2.6 fusion.91
  285.0 5.5 %all_gather.15 = bf16[8,4096]{1,0:T(8,128)(2,1)S(1)} all-gather(bf16[8,1024]{1,0:T(8,128)(2,1)S(1)} %get-tuple-element.599), channel_id=1, replica_groups=mesh['row'=8,'col'=4] {'col'}, dimensions={1}, use_global_device_ids=true | all-gather | bytes 81920 | tf_op jit(solution)/shard_map/all_gather | solution.py:98
  290.5 30.5 %all_gather.14 = bf16[8,8192]{1,0:T(8,128)(2,1)S(1)} all-gather(bf16[8,1024]{1,0:T(8,128)(2,1)S(1)} %get-tuple-element.599), channel_id=1, replica_groups=mesh['row'=8,'col'=4] {'row'}, dimensions={1}, use_global_device_ids=true | all-gather | bytes 147456 | tf_op jit(solution)/shard_map/all_gather | solution.py:99
  321.1 7.7 %while.35 = (s32[]{:T(128)}, f32[8,32,128]{2,1,0:T(8,128)S(1)}, f32[8,64,128]{2,1,0:T(8,128)S(1)}, s32[]{:T(128)}, s32[128]{0:T(128)S(1)}, /*index=5*/bf16[8,64,...) while((s32[]{:T(128)}, f32[8,32,128]{2,1,0:T(8,128)S(1)}, ...), condition=%wide.region_10.17_spmd.clone, body=%wide.region_9.16_spmd.clone.sunk | while | flops 27925444 | bytes 3356565 | solution.py:68
  322.4 0.7 compare_and_fusion.17
  324.4 2.8 gather_fusion.5
  328.8 0.7 copy.70
  329.6 0.9 copy.68
  330.6 1.8 scatter.15
  332.8 69.3 %reduce-scatter.9.cloned.1.call-done = f32[8,1024]{1,0:T(8,128)} async-done(((f32[8,4096]{1,0:T(8,128)}), f32[8,1024]{1,0:T(8,128)}) %reduce-scatter.9.cloned.1.call-update) | async-done | bytes 32784 | tf_op jit(solution)/shard_map/reduce_scatter | solution.py:115
  402.1 65.3 %reduce-scatter.11.cloned.1.call-done = f32[8,1024]{1,0:T(8,128)} async-done(((f32[8,8192]{1,0:T(8,128)}), f32[8,1024]{1,0:T(8,128)}) %reduce-scatter.11.cloned.1.call-update) | async-done | bytes 32784 | tf_op jit(solution)/shard_map/reduce_scatter | solution.py:121
  467.4 1.6 convolution_subtract_fusion.1
  469.3 40.2 %all-reduce.1 = (f32[8,8]{1,0:T(8,128)S(1)}, f32[8,8]{0,1:T(8,128)S(1)}) all-reduce(f32[8,8]{1,0:T(8,128)S(1)} %fusion.104, f32[8,8]{0,1:T(8,128)S(1)} %fusion.103), channel_id=1, replica_groups=mesh['row'=8,'col'=4] {'row','col'}, use_global_device_ids=true, to_apply=%region_14.21 | all-reduce | flops 128 | bytes 1024 | tf_op jit(solution)/shard_map/psum | solution.py:132
  510.4 0.7 cholesky.81
  513.1 0.9 convolution_multiply_fusion
  (82 shorter events, 17.6 us)
Async XLA Ops:
  7.2 2.1 copy-start
  7.2 165.7 %reduce-scatter.5.cloned.1.call-start = ((), (), s32[]{:S(2)}) async-start(), calls=%async_computation.4 | async-start | bytes 163840 | tf_op jit(solution)/shard_map/reduce_scatter | solution.py:115
  99.6 138.7 %reduce-scatter.7.cloned.1.call-start = ((), (), s32[]{:S(2)}) async-start(), calls=%async_computation.5 | async-start | bytes 294912 | tf_op jit(solution)/shard_map/reduce_scatter | solution.py:121
  100.5 301.6 %reduce-scatter.9.cloned.1.call-start = ((), (), s32[]{:S(2)}) async-start(), calls=%async_computation.6 | async-start | bytes 163840 | tf_op jit(solution)/shard_map/reduce_scatter | solution.py:115
  329.6 137.8 %reduce-scatter.11.cloned.1.call-start = ((), (), s32[]{:S(2)}) async-start(), calls=%async_computation.7 | async-start | bytes 294912 | tf_op jit(solution)/shard_map/reduce_scatter | solution.py:121
  510.4 3.6 copy-start.1
Sparse Core Ops, SparseCore 0:
  99.7 73.1 reduce-scatter.4
  176.2 62.0 reduce-scatter.6
  329.7 72.3 reduce-scatter.8
  405.3 62.0 reduce-scatter.10
where the time goes:
time: 522 us; the launch traced here: 521 us
  waiting for transfers between devices  271 us (52%)
  blocking collectives  194 us (37%)
  local copies, waits for them, and re-layouts  19.4 us (4%)
  between operations  14.6 us (3%)
  other arithmetic  13.1 us (3%)
  matrix products  7.66 us (1%)
    reduce_scatter x2, waiting for transfers between devices, per_device(): lax.psum_scatter(row_total.reshape(vectors, row_blocks * block_side), 'co...  140 us
    reduce_scatter x2, waiting for transfers between devices, per_device(): lax.psum_scatter(col_total.reshape(vectors, col_blocks * block_side), 'ro...  131 us
    psum x2, blocking collectives, per_device(): projection, squares = lax.psum((local_proj, local_square), ('row', 'col'))  80.4 us
    all_gather x2, blocking collectives, per_device(): col_vector = lax.all_gather(half_block, 'row', axis=1, tiled=True)  61 us
    psum x1, blocking collectives, per_device(): lax.psum(jnp.dot(start_block, start_block.T, precision=highest), ('row',...  41.9 us
    all_gather x2, blocking collectives, per_device(): row_vector = lax.all_gather(half_block, 'col', axis=1, tiled=True)  11 us
  transfers between devices with their start and end apart: 4, of which 4 were waited for; matrix products, arithmetic and copies ran while one was open for 1% of the time, Pallas kernels for 0%

commit v1 on v0

--- a/solution.py
+++ b/solution.py
@@ -86,7 +86,9 @@
     own_count = counts[tile_row, tile_col]
     own_rows = row_lists[tile_row]
     own_cols = col_lists[tile_row]
-    start_sum = lax.psum(jnp.dot(start_block, start_block.T, precision=highest), ("row", "col"))
+    start_sum = lax.psum(
+        lax.psum(jnp.dot(start_block, start_block.T, precision=highest), "row"), "col"
+    )
     factor = jnp.linalg.cholesky(start_sum)
     current = lax.linalg.triangular_solve(factor, start_block, left_side=True, lower=True)
     previous = current

time: 522 us -> 506 us (0.969)
  blocking collectives: 194 us -> 181 us
    psum x1 -> x2, blocking collectives: 41.9 us -> 28.8 us  [the longest x1 23.1 us: per_device(): lax.psum(jnp.dot(start_block, start_block.T, precision=highest), 'row')]
where the time goes in v1:
time: 506 us; the launch traced here: 504 us
  waiting for transfers between devices  269 us (53%)
  blocking collectives  181 us (36%)
  local copies, waits for them, and re-layouts  19.4 us (4%)
  between operations  14.6 us (3%)
  other arithmetic  13.1 us (3%)
  matrix products  7.65 us (2%)
    reduce_scatter x2, waiting for transfers between devices, per_device(): lax.psum_scatter(row_total.reshape(vectors, row_blocks * block_side), 'co...  138 us
    reduce_scatter x2, waiting for transfers between devices, per_device(): lax.psum_scatter(col_total.reshape(vectors, col_blocks * block_side), 'ro...  131 us
    psum x2, blocking collectives, per_device(): projection, squares = lax.psum((local_proj, local_square), ('row', 'col'))  80.3 us
    all_gather x2, blocking collectives, per_device(): col_vector = lax.all_gather(half_block, 'row', axis=1, tiled=True)  61 us
    psum x1, blocking collectives, per_device(): lax.psum(jnp.dot(start_block, start_block.T, precision=highest), 'row')  23.1 us
    all_gather x2, blocking collectives, per_device(): row_vector = lax.all_gather(half_block, 'col', axis=1, tiled=True)  10.7 us
  transfers between devices with their start and end apart: 4, of which 4 were waited for; matrix products, arithmetic and copies ran while one was open for 1% of the time, Pallas kernels for 0%

profile of v1, /device:TPU:0, one launch (start us, length us, event | category | flops | bytes accessed | tf_op | source)
XLA Modules:
  0.0 504.5 jit_solution(1432146174159704399)
XLA Ops:
  7.2 1.3 dynamic_slice.9
  9.4 23.1 %psum.42 = f32[8,8]{0,1:T(8,128)S(1)} all-reduce(f32[8,8]{0,1:T(8,128)S(1)} %fusion.100), channel_id=1, replica_groups=mesh['row'=8,'col'=4] {'row'}, use_global_device_ids=true, to_apply=%region_0.0 | all-reduce | flops 64 | bytes 512 | tf_op jit(solution)/shard_map/psum | solution.py:90
  32.6 5.7 %psum.43 = f32[8,8]{0,1:T(8,128)S(1)} all-reduce(f32[8,8]{0,1:T(8,128)S(1)} %psum.42), channel_id=1, replica_groups=mesh['row'=8,'col'=4] {'col'}, use_global_device_ids=true, to_apply=%region_1.0 | all-reduce | flops 64 | bytes 512 | tf_op jit(solution)/shard_map/psum | solution.py:89
  38.3 0.7 cholesky.59
  41.2 5.2 %all_gather.13 = bf16[8,4096]{1,0:T(8,128)(2,1)S(1)} all-gather(bf16[8,1024]{1,0:T(8,128)(2,1)S(1)} %get-tuple-element.597), channel_id=1, replica_groups=mesh['row'=8,'col'=4] {'col'}, dimensions={1}, use_global_device_ids=true | all-gather | bytes 81920 | tf_op jit(solution)/shard_map/all_gather | solution.py:100
  46.5 30.5 %all_gather.12 = bf16[8,8192]{1,0:T(8,128)(2,1)S(1)} all-gather(bf16[8,1024]{1,0:T(8,128)(2,1)S(1)} %get-tuple-element.597), channel_id=1, replica_groups=mesh['row'=8,'col'=4] {'row'}, dimensions={1}, use_global_device_ids=true | all-gather | bytes 147456 | tf_op jit(solution)/shard_map/all_gather | solution.py:101
  77.7 7.7 %while.34 = (s32[]{:T(128)}, f32[8,32,128]{2,1,0:T(8,128)S(1)}, f32[8,64,128]{2,1,0:T(8,128)S(1)}, s32[]{:T(128)}, s32[128]{0:T(128)S(1)}, /*index=5*/bf16[8,64,...) while((s32[]{:T(128)}, f32[8,32,128]{2,1,0:T(8,128)S(1)}, ...), condition=%wide.region_5.12_spmd.clone, body=%wide.region_4.11_spmd.clone.sunk | while | flops 27925444 | bytes 3356565 | solution.py:68
  79.1 0.7 compare_and_fusion.14
  81.0 2.8 gather_fusion
  85.4 0.7 copy.71
  86.2 0.8 copy.69
  87.2 0.7 and_reduce_fusion
  88.5 68.4 %reduce-scatter.5.cloned.1.call-done = f32[8,1024]{1,0:T(8,128)} async-done(((f32[8,4096]{1,0:T(8,128)}), f32[8,1024]{1,0:T(8,128)}) %reduce-scatter.5.cloned.1.call-update) | async-done | bytes 32784 | tf_op jit(solution)/shard_map/reduce_scatter | solution.py:117
  157.0 65.4 %reduce-scatter.7.cloned.1.call-done = f32[8,1024]{1,0:T(8,128)} async-done(((f32[8,8192]{1,0:T(8,128)}), f32[8,1024]{1,0:T(8,128)}) %reduce-scatter.7.cloned.1.call-update) | async-done | bytes 32784 | tf_op jit(solution)/shard_map/reduce_scatter | solution.py:123
  222.4 0.8 add.230
  223.5 40.1 %all-reduce.2 = (f32[8,8]{1,0:T(8,128)S(1)}, f32[8,8]{0,1:T(8,128)S(1)}) all-reduce(f32[8,8]{1,0:T(8,128)S(1)} %fusion.102, f32[8,8]{0,1:T(8,128)S(1)} %fusion.101), channel_id=1, replica_groups=mesh['row'=8,'col'=4] {'row','col'}, use_global_device_ids=true, to_apply=%region_9.16 | all-reduce | flops 128 | bytes 1024 | tf_op jit(solution)/shard_map/psum | solution.py:134
  264.1 0.7 cholesky.70
  265.6 2.6 fusion.91
  269.0 5.5 %all_gather.15 = bf16[8,4096]{1,0:T(8,128)(2,1)S(1)} all-gather(bf16[8,1024]{1,0:T(8,128)(2,1)S(1)} %get-tuple-element.599), channel_id=1, replica_groups=mesh['row'=8,'col'=4] {'col'}, dimensions={1}, use_global_device_ids=true | all-gather | bytes 81920 | tf_op jit(solution)/shard_map/all_gather | solution.py:100
  274.5 30.5 %all_gather.14 = bf16[8,8192]{1,0:T(8,128)(2,1)S(1)} all-gather(bf16[8,1024]{1,0:T(8,128)(2,1)S(1)} %get-tuple-element.599), channel_id=1, replica_groups=mesh['row'=8,'col'=4] {'row'}, dimensions={1}, use_global_device_ids=true | all-gather | bytes 147456 | tf_op jit(solution)/shard_map/all_gather | solution.py:101
  305.1 7.7 %while.35 = (s32[]{:T(128)}, f32[8,32,128]{2,1,0:T(8,128)S(1)}, f32[8,64,128]{2,1,0:T(8,128)S(1)}, s32[]{:T(128)}, s32[128]{0:T(128)S(1)}, /*index=5*/bf16[8,64,...) while((s32[]{:T(128)}, f32[8,32,128]{2,1,0:T(8,128)S(1)}, ...), condition=%wide.region_11.18_spmd.clone, body=%wide.region_10.17_spmd.clone.sunk | while | flops 27925444 | bytes 3356565 | solution.py:68
  306.5 0.7 compare_and_fusion.17
  308.4 2.8 gather_fusion.5
  312.8 0.7 copy.70
  313.6 0.9 copy.68
  314.6 1.8 scatter.15
  316.8 69.3 %reduce-scatter.9.cloned.1.call-done = f32[8,1024]{1,0:T(8,128)} async-done(((f32[8,4096]{1,0:T(8,128)}), f32[8,1024]{1,0:T(8,128)}) %reduce-scatter.9.cloned.1.call-update) | async-done | bytes 32784 | tf_op jit(solution)/shard_map/reduce_scatter | solution.py:117
  386.1 65.2 %reduce-scatter.11.cloned.1.call-done = f32[8,1024]{1,0:T(8,128)} async-done(((f32[8,8192]{1,0:T(8,128)}), f32[8,1024]{1,0:T(8,128)}) %reduce-scatter.11.cloned.1.call-update) | async-done | bytes 32784 | tf_op jit(solution)/shard_map/reduce_scatter | solution.py:123
  451.4 1.6 convolution_subtract_fusion.1
  453.3 40.1 %all-reduce.1 = (f32[8,8]{1,0:T(8,128)S(1)}, f32[8,8]{0,1:T(8,128)S(1)}) all-reduce(f32[8,8]{1,0:T(8,128)S(1)} %fusion.104, f32[8,8]{0,1:T(8,128)S(1)} %fusion.103), channel_id=1, replica_groups=mesh['row'=8,'col'=4] {'row','col'}, use_global_device_ids=true, to_apply=%region_15.22 | all-reduce | flops 128 | bytes 1024 | tf_op jit(solution)/shard_map/psum | solution.py:134
  494.4 0.7 cholesky.81
  497.1 0.9 convolution_multiply_fusion
  (83 shorter events, 18.3 us)
Async XLA Ops:
  7.2 2.1 copy-start
  7.2 149.8 %reduce-scatter.5.cloned.1.call-start = ((), (), s32[]{:S(2)}) async-start(), calls=%async_computation.4 | async-start | bytes 163840 | tf_op jit(solution)/shard_map/reduce_scatter | solution.py:117
  86.2 136.2 %reduce-scatter.7.cloned.1.call-start = ((), (), s32[]{:S(2)}) async-start(), calls=%async_computation.5 | async-start | bytes 294912 | tf_op jit(solution)/shard_map/reduce_scatter | solution.py:123
  87.1 299.0 %reduce-scatter.9.cloned.1.call-start = ((), (), s32[]{:S(2)}) async-start(), calls=%async_computation.6 | async-start | bytes 163840 | tf_op jit(solution)/shard_map/reduce_scatter | solution.py:117
  313.6 137.8 %reduce-scatter.11.cloned.1.call-start = ((), (), s32[]{:S(2)}) async-start(), calls=%async_computation.7 | async-start | bytes 294912 | tf_op jit(solution)/shard_map/reduce_scatter | solution.py:123
  494.3 3.6 copy-start.1
Sparse Core Ops, SparseCore 0:
  86.3 70.6 reduce-scatter.4
  160.3 62.0 reduce-scatter.6
  313.7 72.3 reduce-scatter.8
  389.3 62.0 reduce-scatter.10
